TPU v7x, 32 devices: a whole 2x2x4 slice. The times are simulated.
32 devices in a mesh: group: 2 (over x), shard: 16 (over z, y, core).
Axes of the slice: x: 2, y: 2, z: 4, core: 2. Of those that a mesh axis runs over, the one named last changes fastest.
Arguments:
- rollout_rows: bfloat16 [512, 8192], P('group', 'shard'), may hold values from -6 to 6
- assign: int32 [512], replicated, may hold values from 0 to 511, each once
- cotangent: bfloat16 [512, 8192], P('group', 'shard'), may hold values from -3 to 3
- w_master: float32 [8192, 8192], P('group', 'shard'), may hold values from -0.0625 to 0.0625
- adam_m: float32 [8192, 8192], P('group', 'shard'), may hold values from -6 to 6
- adam_v: float32 [8192, 8192], P('group', 'shard'), may hold values from 0.05 to 1
- tile_mask: int32 [64, 64], replicated, may hold values from 0 to 1, as said below
Outputs:
- projected: bfloat16 [512, 8192], P('group', 'shard')
- input_grad: bfloat16 [512, 8192], P('group', 'shard')
- w_updated: float32 [8192, 8192], P('group', 'shard')
- m_updated: float32 [8192, 8192], P('group', 'shard')
- v_updated: float32 [8192, 8192], P('group', 'shard')
- rollout_tiles: bfloat16 [64, 6, 128, 128], P('shard')
Inputs may be any that keep to these rules, and one draw needn't show every extreme that they name: `tile_mask`: each tile column has 1 to 6 trainable tiles, and some column has exactly 6. `assign`: a permutation of the 512 rollout rows.
All inputs are finite; a program needn't handle non-finite values.
Results may differ from a plain program's by a relative error of at most 0.0051.
Values may be sent and summed in bfloat16 or wider, within the bound.
No kernel may reach another device: no remote copies, remote signals or barrier semaphores. Data moves between devices by JAX's collectives and lax.ppermute only.
A program may use at most 192 MiB of HBM per device.

v0:
```python
import jax
import jax.numpy as jnp
from jax import lax
from jax.sharding import PartitionSpec as P

TILE = 128
CAP = 6
beta_one = 0.9
beta_two = 0.999
learn_rate = 0.02
eps_adam = 1e-08
bias_one = 1.0 - 0.9**10
bias_two = 1.0 - 0.999**10


def shards(rollout_rows, assign, cotangent, w_master, adam_m, adam_v, tile_mask):
    group_at = lax.axis_index("group")
    shard_at = lax.axis_index("shard")
    row_count = cotangent.shape[0]
    col_tiles = cotangent.shape[1] // TILE
    row_tiles = w_master.shape[0] // TILE
    w_half = w_master.astype(jnp.bfloat16)
    all_rows, w_cols = (
        lax.all_gather(rollout_rows, "group", axis=0, tiled=True),
        lax.all_gather(w_half, "group", axis=0, tiled=True),
    )
    my_rows = lax.dynamic_slice_in_dim(assign, group_at * row_count, row_count)
    picked = jnp.take(all_rows, my_rows, axis=0)
    x_full, dy_full = (
        lax.all_gather(picked, "shard", axis=1, tiled=True),
        lax.all_gather(cotangent, "shard", axis=1, tiled=True),
    )
    projected = jnp.dot(x_full, w_cols, preferred_element_type=jnp.float32).astype(jnp.bfloat16)
    w_rows = lax.all_to_all(w_cols, "shard", split_axis=0, concat_axis=1, tiled=True)
    input_grad = lax.dot_general(
        dy_full, w_rows, (((1,), (1,)), ((), ())), preferred_element_type=jnp.float32
    ).astype(jnp.bfloat16)
    mask_cols = lax.dynamic_slice_in_dim(tile_mask, shard_at * col_tiles, col_tiles, 1)
    row_order = jnp.argsort(1 - mask_cols, axis=0, stable=True)
    slot_index = row_order[:CAP].T
    counts = jnp.sum(mask_cols, axis=0)
    live_slot = jnp.arange(CAP)[None, :] < counts[:, None]
    owner_rows = group_at * row_tiles + jnp.arange(row_tiles)
    owner_map = (
        (slot_index[:, :, None] == owner_rows[None, None, :]) & live_slot[:, :, None]
    ).astype(jnp.float32)
    partial_value = lax.dot_general(
        x_full, cotangent, (((0,), (0,)), ((), ())), preferred_element_type=jnp.float32
    )
    gradient = lax.psum_scatter(
        partial_value.astype(jnp.bfloat16), "group", scatter_dimension=0, tiled=True
    ).astype(jnp.float32)
    mask_local = (
        lax.dynamic_slice(
            tile_mask, (group_at * row_tiles, shard_at * col_tiles), (row_tiles, col_tiles)
        )
        > 0
    )
    mask_wide = jnp.broadcast_to(
        mask_local[:, None, :, None], (row_tiles, TILE, col_tiles, TILE)
    ).reshape(w_master.shape)
    m_updated = jnp.where(mask_wide, beta_one * adam_m + (1.0 - beta_one) * gradient, adam_m)
    v_updated = jnp.where(
        mask_wide, beta_two * adam_v + (1.0 - beta_two) * gradient * gradient, adam_v
    )
    adam_step = m_updated / bias_one / (jnp.sqrt(v_updated / bias_two) + eps_adam)
    w_updated = jnp.where(mask_wide, w_master - learn_rate * adam_step, w_master)
    new_tiles = w_updated.reshape(row_tiles, TILE, col_tiles, TILE).transpose(0, 2, 1, 3)
    fresh_terms = jnp.einsum(
        "cjk,kcab->cjab", owner_map, new_tiles, precision=lax.Precision.HIGHEST
    )
    rollout_tiles = lax.psum(fresh_terms.astype(jnp.bfloat16), "group")
    return (projected, input_grad, w_updated, m_updated, v_updated, rollout_tiles)


def solution(mesh):
    placed = (
        P("group", "shard"),
        P(),
        P("group", "shard"),
        P("group", "shard"),
        P("group", "shard"),
        P("group", "shard"),
        P(),
    )
    return jax.shard_map(
        shards,
        mesh=mesh,
        in_specs=placed,
        out_specs=(
            P("group", "shard"),
            P("group", "shard"),
            P("group", "shard"),
            P("group", "shard"),
            P("group", "shard"),
            P("shard", None, None, None),
        ),
        check_vma=False,
    )
```

profile of v0, /device:TPU:13, one launch (start us, length us, event | category | flops | bytes accessed | tf_op | source)
XLA Modules:
  0.0 546.4 jit_solution(14071634290224153602)
XLA Ops:
  7.2 0.0 all-gather.4.cloned.1.call-start
  7.2 0.8 compare_and_fusion
  8.0 8.1 %all_gather.12 = bf16[512,512]{1,0:T(8,128)(2,1)S(1)} all-gather(bf16[256,512]{1,0:T(8,128)(2,1)} %param.7), channel_id=1, replica_groups=mesh['group'=2,'shard'=16] {'group'}, dimensions={0}, use_global_device_ids=true | all-gather | bytes 786432 | tf_op jit(solution)/shard_map/all_gather | solution.py:24
  16.1 1.2 gather_fusion
  17.2 0.8 broadcast_select_fusion
  18.0 0.0 all-gather.4.cloned.1.call-update
  18.0 0.0 copy-start
  18.1 0.0 reduce-scatter.2.cloned.1.call-start
  18.1 52.3 %all-gather.4.cloned.1.call-done = bf16[256,8192]{1,0:T(8,128)(2,1)} async-done(((bf16[256,512]{1,0:T(8,128)(2,1)}), bf16[256,8192]{1,0:T(8,128)(2,1)}) %all-gather.4.cloned.1.call-update) | async-done | bytes 4194320 | tf_op jit(solution)/shard_map/all_gather | solution.py:30
  70.4 8.0 %convolution_convert_fusion = bf16[8192,512]{1,0:T(8,128)(2,1)} fusion(bf16[256,8192]{1,0:T(8,128)(2,1)} %all-gather.4.cloned.1.call-done, bf16[256,512]{1,0:T(8,128)(2,1)} %param.9), kind=kOutput, calls=%fused_computation.3 | convolution fusion | flops 2151677952 | bytes 12845056 | tf_op jit(solution)/shard_map/dot_general | solution.py:47
  78.4 0.0 reduce-scatter.2.cloned.1.call-update
  78.5 0.0 all-gather.6.cloned.1.call-start
  78.5 0.0 copy-done
  78.5 0.1 dynamic-slice_compare_fusion
  78.6 99.5 %reduce-scatter.2.cloned.1.call-done = bf16[4096,512]{1,0:T(8,128)(2,1)} async-done(((bf16[8192,512]{1,0:T(8,128)(2,1)}), bf16[4096,512]{1,0:T(8,128)(2,1)}) %reduce-scatter.2.cloned.1.call-update) | async-done | bytes 4194320 | tf_op jit(solution)/shard_map/reduce_scatter | solution.py:50
  178.1 1.1 broadcast_in_dim.26
  179.3 22.2 %subtract_select_fusion = (f32[4096,512]{1,0:T(8,128)}, f32[4096,512]{1,0:T(8,128)}, f32[4096,512]{1,0:T(8,128)}, bf16[4096,512]{1,0:T(8,128)(2,1)}) fusion(f32[4096,512]{1,0:T(8,128)} %param.10, pred[512,8,4,128]{3,2,1,0:T(4,128)(4,1)S(1)} %bitcast.31, f32[4096,512]{1,0:T(8,128)} %param.11, bf16[4096,512]{1,0:T(8,128)(2,1)} %reduce-scatter.2.cloned.1.call-done, ...), kind=kLoop, calls=%fused_computation.1 | loop fusion | flops 37748736 | bytes 60817408 | tf_op jit(solution)/shard_map/jit(_where)/select_n | solution.py:67
  201.5 0.0 all-gather.6.cloned.1.call-update
  201.5 104.2 %all-gather.6.cloned.1.call-done = bf16[8192,512]{1,0:T(8,128)(2,1)} async-done(((bf16[4096,512]{1,0:T(8,128)(2,1)}), bf16[8192,512]{1,0:T(8,128)(2,1)}) %all-gather.6.cloned.1.call-update) | async-done | bytes 8388624 | tf_op jit(solution)/shard_map/all_gather | solution.py:25
  305.6 6.5 %all-to-all-start = ((bf16[16,512,512]{2,1,0:T(8,128)(2,1)}), bf16[16,512,512]{2,1,0:T(8,128)(2,1)}, u32[]{:S(2)}, u32[]{:S(2)}) async-start(bf16[16,512,512]{2,1,0:T(8,128)(2,1)} %bitcast.29), calls=%async_computation | async-start | bytes 16777216 | tf_op jit(solution)/shard_map/all_to_all | solution.py:34
  312.1 0.2 all-reduce.2.cloned.1.call-start
  312.4 0.1 dynamic-slice_reduce_fusion
  312.5 1.0 sort.17
  313.5 0.1 copy.19
  313.6 0.1 iota_compare_fusion
  313.7 9.9 %reshape.54 = f32[32,128,4,128]{3,2,1,0:T(4,128)} reshape(f32[4096,512]{1,0:T(8,128)} %get-tuple-element.26) | data formatting | bytes 16777216 | tf_op jit(solution)/shard_map/reshape | solution.py:68
  323.6 11.6 %fusion.7 = bf16[4,6,128,128]{3,1,2,0:T(8,128)(2,1)} fusion(f32[32,128,4,128]{3,2,1,0:T(4,128)} %reshape.54, s32[32]{0:T(128)S(1)} %iota_add_fusion, s32[4,6]{1,0:T(4,128)S(1)} %copy.19, pred[4,6]{1,0:T(4,128)(4,1)S(1)} %iota_compare_fusion), kind=kOutput, calls=%fused_computation.12 | convolution fusion | flops 151389696 | bytes 9175288 | tf_op jit(solution)/shard_map/cjk,kcab->cjab/dot_general | solution.py:69
  335.1 0.0 all-reduce.2.cloned.1.call-update
  335.2 0.0 all-gather.8.cloned.1.call-start
  335.2 0.5 all-gather.8.cloned.1.call-update
  335.8 39.2 %all-reduce.2.cloned.1.call-done = bf16[4,6,128,128]{3,1,2,0:T(8,128)(2,1)} async-done(((bf16[4,6,128,128]{3,1,2,0:T(8,128)(2,1)}), bf16[4,6,128,128]{3,1,2,0:T(8,128)(2,1)}) %all-reduce.2.cloned.1.call-update) | async-done | bytes 786448 | tf_op jit(solution)/shard_map/psum | solution.py:72
  374.9 2.3 copy.21
  377.2 7.7 %convolution_convert_fusion.2 = bf16[256,512]{1,0:T(8,128)(2,1)} fusion(bf16[256,8192]{1,0:T(8,128)(2,1)} %all-gather.4.cloned.1.call-done, bf16[8192,512]{1,0:T(8,128)(2,1)} %all-gather.6.cloned.1.call-done), kind=kOutput, calls=%fused_computation.14 | convolution fusion | flops 2147614720 | bytes 12845056 | tf_op jit(solution)/shard_map/dot_general | solution.py:33
  384.9 135.0 %all-to-all-done = bf16[16,512,512]{2,1,0:T(8,128)(2,1)} async-done(((bf16[16,512,512]{2,1,0:T(8,128)(2,1)}), bf16[16,512,512]{2,1,0:T(8,128)(2,1)}, u32[]{:S(2)}, u32[]{:S(2)}) %all-to-all-start) | async-done | bytes 8388640 | tf_op jit(solution)/shard_map/all_to_all | solution.py:34
  519.9 12.3 %copy.18 = bf16[512,16,512]{0,2,1:T(8,128)(2,1)} copy(bf16[512,16,512]{2,0,1:T(8,128)(2,1)} %bitcast.1) | data formatting | bytes 16777216 | tf_op jit(solution)/shard_map/all_to_all | solution.py:34
  532.2 0.0 all-gather.8.cloned.1.call-done
  532.2 7.7 %convolution_convert_fusion.1 = bf16[256,512]{1,0:T(8,128)(2,1)} fusion(bf16[256,8192]{1,0:T(8,128)(2,1)} %all-gather.8.cloned.1.call-done, bf16[512,8192]{0,1:T(8,128)(2,1)} %bitcast.30), kind=kOutput, calls=%fused_computation.13 | convolution fusion | flops 2147614720 | bytes 12845056 | tf_op jit(solution)/shard_map/dot_general | solution.py:35
  (4 shorter events, 0.0 us)
Async XLA Ops:
  7.2 63.3 %all-gather.4.cloned.1.call-start = ((), (), s32[]{:S(2)}) async-start(), calls=%async_computation.2 | async-start | bytes 4456448 | tf_op jit(solution)/shard_map/all_gather | solution.py:30
  18.0 60.5 %copy-start = (s32[64,64]{1,0:T(8,128)S(1)}, s32[64,64]{1,0:T(8,128)}, u32[]{:S(2)}) copy-start(s32[64,64]{1,0:T(8,128)} %param.13) | copy-start | bytes 49156
  18.1 160.1 %reduce-scatter.2.cloned.1.call-start = ((), (), s32[]{:S(2)}) async-start(), calls=%async_computation.5 | async-start | bytes 12582912 | tf_op jit(solution)/shard_map/reduce_scatter | solution.py:50
  78.5 227.2 %all-gather.6.cloned.1.call-start = ((), (), s32[]{:S(2)}) async-start(), calls=%async_computation.3 | async-start | bytes 12582912 | tf_op jit(solution)/shard_map/all_gather | solution.py:25
  305.6 214.2 %all-to-all-start = ((bf16[16,512,512]{2,1,0:T(8,128)(2,1)}), bf16[16,512,512]{2,1,0:T(8,128)(2,1)}, u32[]{:S(2)}, u32[]{:S(2)}) async-start(bf16[16,512,512]{2,1,0:T(8,128)(2,1)} %bitcast.29), calls=%async_computation | async-start | bytes 16777216 | tf_op jit(solution)/shard_map/all_to_all | solution.py:34
  312.1 62.8 %all-reduce.2.cloned.1.call-start = ((), (), s32[]{:S(2)}) async-start(), calls=%async_computation.6 | async-start | bytes 2097152 | tf_op jit(solution)/shard_map/psum | solution.py:72
  335.2 197.0 %all-gather.8.cloned.1.call-start = ((), (), s32[]{:S(2)}) async-start(), calls=%async_computation.4 | async-start | bytes 4456448 | tf_op jit(solution)/shard_map/all_gather | solution.py:31
Sparse Core Ops, SparseCore 0:
  18.2 52.2 all-gather.3
  78.6 99.5 reduce-scatter.1
  201.6 103.9 all-gather.5
  335.3 39.5 all-reduce.1
  376.9 115.9 all-gather.7
where the time goes:
time: 547 us; the launch traced here: 546 us
  waiting for transfers between devices  431 us (79%)
  matrix products  34.9 us (6%)
  local copies, waits for them, and re-layouts  26.9 us (5%)
  other arithmetic  25 us (5%)
  between operations  13.8 us (3%)
  blocking collectives  8.06 us (1%)
  starting transfers between devices  6.89 us (1%)
    all_to_all x1, waiting for transfers between devices, shards(): lax.all_to_all(w_cols, 'shard', split_axis=0, concat_axis=1, tiled=True)  135 us
    all_gather x1, waiting for transfers between devices, shards(): lax.all_gather(w_half, 'group', axis=0, tiled=True)  104 us
    reduce_scatter x1, waiting for transfers between devices, shards(): lax.psum_scatter(partial_value.astype(jnp.bfloat16), 'group', scatter_dim...  99.5 us
    all_gather x1, waiting for transfers between devices, shards(): lax.all_gather(picked, 'shard', axis=1, tiled=True)  52.3 us
    psum x1, waiting for transfers between devices, shards(): rollout_tiles = lax.psum(fresh_terms.astype(jnp.bfloat16), 'group')  39.2 us
    select_n x1, other arithmetic, shards(): jnp.where(mask_wide, w_master - learn_rate * adam_step, w_master)  22.2 us
    all_to_all x1, local copies, waits for them, and re-layouts, shards(): lax.all_to_all(w_cols, 'shard', split_axis=0, concat_axis=1, tiled=True)  12.3 us
    dot_general x1, matrix products, shards(): jnp.einsum('cjk,kcab->cjab', owner_map, new_tiles, precision=lax.Precisio...  11.6 us
  transfers between devices with their start and end apart: 6, of which 5 were waited for; matrix products, arithmetic and copies ran while one was open for 8% of the time, Pallas kernels for 0%

commit v1 on v0

--- a/solution.py
+++ b/solution.py
@@ -31,7 +31,10 @@
         lax.all_gather(cotangent, "shard", axis=1, tiled=True),
     )
     projected = jnp.dot(x_full, w_cols, preferred_element_type=jnp.float32).astype(jnp.bfloat16)
-    w_rows = lax.all_to_all(w_cols, "shard", split_axis=0, concat_axis=1, tiled=True)
+    w_rows = jnp.concatenate(
+        lax.all_to_all(jnp.stack(jnp.split(w_cols, lax.axis_size("shard"), axis=0)), "shard", 0, 0),
+        axis=1,
+    )
     input_grad = lax.dot_general(
         dy_full, w_rows, (((1,), (1,)), ((), ())), preferred_element_type=jnp.float32
     ).astype(jnp.bfloat16)

time: 547 us -> 449 us (0.82)
  waiting for transfers between devices: 431 us -> 305 us
  local copies, waits for them, and re-layouts: 26.9 us -> 53 us
    all_to_all x1, waiting for transfers between devices: 135 us -> 26.9 us  [shards(): lax.all_to_all(jnp.stack(jnp.split(w_cols, lax.axis_size('shard'), axis=0...]
    all_gather x1, waiting for transfers between devices: 0.01 us -> 70.7 us  [shards(): lax.all_gather(cotangent, 'shard', axis=1, tiled=True)]
    reduce_scatter x1, waiting for transfers between devices: 99.5 us -> 55.3 us  [shards(): lax.psum_scatter(partial_value.astype(jnp.bfloat16), 'group', scatter_dim...]
    unnamed x3 -> x22, local copies, waits for them, and re-layouts: 2.28 us -> 38.7 us
    psum x1, waiting for transfers between devices: 39.2 us -> 7.91 us  [shards(): rollout_tiles = lax.psum(fresh_terms.astype(jnp.bfloat16), 'group')]
    all_to_all x1 -> x0, local copies, waits for them, and re-layouts: 12.3 us -> none  [shards(): lax.all_to_all(w_cols, 'shard', split_axis=0, concat_axis=1, tiled=True)]
    all_gather x1, waiting for transfers between devices: 52.3 us -> 45 us  [shards(): lax.all_gather(picked, 'shard', axis=1, tiled=True)]
    all_gather x1, waiting for transfers between devices: 104 us -> 98.4 us  [shards(): lax.all_gather(w_half, 'group', axis=0, tiled=True)]
  transfers between devices with their start and end apart: 6 -> 6, of which waited for: 5 -> 6; matrix products, arithmetic and copies ran while one was open for 8% -> 24% of each run, Pallas kernels for 0% -> 0%
where the time goes in v1:
time: 449 us; the launch traced here: 446 us
  waiting for transfers between devices  305 us (68%)
  local copies, waits for them, and re-layouts  53 us (12%)
  matrix products  34.9 us (8%)
  other arithmetic  24.8 us (6%)
  between operations  13.8 us (3%)
  blocking collectives  8.06 us (2%)
  starting transfers between devices  6.85 us (2%)
    all_gather x1, waiting for transfers between devices, shards(): lax.all_gather(w_half, 'group', axis=0, tiled=True)  98.4 us
    all_gather x1, waiting for transfers between devices, shards(): lax.all_gather(cotangent, 'shard', axis=1, tiled=True)  70.7 us
    reduce_scatter x1, waiting for transfers between devices, shards(): lax.psum_scatter(partial_value.astype(jnp.bfloat16), 'group', scatter_dim...  55.3 us
    all_gather x1, waiting for transfers between devices, shards(): lax.all_gather(picked, 'shard', axis=1, tiled=True)  45 us
    unnamed x22, local copies, waits for them, and re-layouts  38.7 us
    all_to_all x1, waiting for transfers between devices, shards(): lax.all_to_all(jnp.stack(jnp.split(w_cols, lax.axis_size('shard'), axis=0...  26.9 us
    select_n x1, other arithmetic, shards(): jnp.where(mask_wide, w_master - learn_rate * adam_step, w_master)  22 us
    dot_general x1, matrix products, shards(): jnp.einsum('cjk,kcab->cjab', owner_map, new_tiles, precision=lax.Precisio...  11.6 us
  transfers between devices with their start and end apart: 6, of which 6 were waited for; matrix products, arithmetic and copies ran while one was open for 24% of the time, Pallas kernels for 0%

profile of v1, /device:TPU:13, one launch (start us, length us, event | category | flops | bytes accessed | tf_op | source)
XLA Modules:
  0.0 446.1 jit_solution(8407651596693543842)
XLA Ops:
  7.2 0.0 all-gather.4.cloned.1.call-start
  7.2 8.1 %all_gather.12 = bf16[512,512]{1,0:T(8,128)(2,1)S(1)} all-gather(bf16[256,512]{1,0:T(8,128)(2,1)} %param.7), channel_id=1, replica_groups=mesh['group'=2,'shard'=16] {'group'}, dimensions={0}, use_global_device_ids=true | all-gather | bytes 786432 | tf_op jit(solution)/shard_map/all_gather | solution.py:24
  15.3 0.8 compare_and_fusion
  16.0 1.2 gather_fusion
  17.2 0.8 broadcast_select_fusion
  18.0 0.0 all-gather.4.cloned.1.call-update
  18.0 0.0 copy-start
  18.0 0.0 all-gather.6.cloned.1.call-start
  18.1 7.3 %copy.16 = bf16[4096,512]{0,1:T(8,128)(2,1)} copy(f32[4096,512]{1,0:T(8,128)} %param.10) | data formatting | bytes 12582912 | tf_op args[3]
  25.4 0.0 all-gather.6.cloned.1.call-update
  25.4 0.0 reduce-scatter.2.cloned.1.call-start
  25.4 45.0 %all-gather.4.cloned.1.call-done = bf16[256,8192]{1,0:T(8,128)(2,1)} async-done(((bf16[256,512]{1,0:T(8,128)(2,1)}), bf16[256,8192]{1,0:T(8,128)(2,1)}) %all-gather.4.cloned.1.call-update) | async-done | bytes 4194320 | tf_op jit(solution)/shard_map/all_gather | solution.py:30
  70.4 0.0 copy-done
  70.4 8.0 %convolution_convert_fusion = bf16[8192,512]{1,0:T(8,128)(2,1)} fusion(bf16[256,8192]{1,0:T(8,128)(2,1)} %all-gather.4.cloned.1.call-done, bf16[256,512]{1,0:T(8,128)(2,1)S(1)} %copy-done), kind=kOutput, calls=%fused_computation.3 | convolution fusion | flops 2151677952 | bytes 12845056 | tf_op jit(solution)/shard_map/dot_general | solution.py:50
  78.4 0.0 reduce-scatter.2.cloned.1.call-update
  78.4 98.4 %all-gather.6.cloned.1.call-done = bf16[8192,512]{0,1:T(8,128)(2,1)} async-done(((bf16[4096,512]{0,1:T(8,128)(2,1)}), bf16[8192,512]{0,1:T(8,128)(2,1)}) %all-gather.6.cloned.1.call-update) | async-done | bytes 8388624 | tf_op jit(solution)/shard_map/all_gather | solution.py:25
  176.8 1.9 fusion.26
  178.7 1.9 fusion.25
  180.5 1.9 fusion.24
  182.4 1.9 fusion.23
  184.3 1.9 fusion.22
  186.1 2.0 fusion.21
  188.2 1.9 fusion.20
  190.0 1.9 fusion.19
  191.9 1.9 fusion.18
  193.8 1.9 fusion.17
  195.7 1.9 fusion.16
  197.6 1.9 fusion.15
  199.5 1.9 fusion.14
  201.4 1.9 fusion.13
  203.3 1.8 fusion.12
  205.1 2.0 fusion.11
  207.1 0.0 copy-start.1
  207.1 6.5 %all-to-all-start = ((bf16[16,512,512]{1,2,0:T(8,128)(2,1)}), bf16[16,512,512]{1,2,0:T(8,128)(2,1)}, u32[]{:S(2)}, u32[]{:S(2)}) async-start(bf16[16,512,512]{1,2,0:T(8,128)(2,1)} %fusion.11), calls=%async_computation | async-start | bytes 16777216 | tf_op jit(solution)/shard_map/all_to_all | solution.py:35
  213.5 0.0 all-gather.8.cloned.1.call-start
  213.6 0.5 all-gather.8.cloned.1.call-update
  214.1 0.2 all-reduce.2.cloned.1.call-start
  214.3 0.0 copy-done.1
  214.4 0.1 dynamic-slice_reduce_fusion
  214.5 1.0 sort.17
  215.5 0.1 copy.17
  215.6 0.1 dynamic-slice_compare_fusion
  215.7 0.1 iota_compare_fusion
  215.7 8.0 %convolution_convert_fusion.2 = bf16[256,512]{1,0:T(8,128)(2,1)} fusion(bf16[256,8192]{1,0:T(8,128)(2,1)} %all-gather.4.cloned.1.call-done, bf16[8192,512]{0,1:T(8,128)(2,1)} %all-gather.6.cloned.1.call-done), kind=kOutput, calls=%fused_computation.14 | convolution fusion | flops 2147614720 | bytes 12845056 | tf_op jit(solution)/shard_map/dot_general | solution.py:33
  223.7 55.3 %reduce-scatter.2.cloned.1.call-done = bf16[4096,512]{1,0:T(8,128)(2,1)} async-done(((bf16[8192,512]{1,0:T(8,128)(2,1)}), bf16[4096,512]{1,0:T(8,128)(2,1)}) %reduce-scatter.2.cloned.1.call-update) | async-done | bytes 4194320 | tf_op jit(solution)/shard_map/reduce_scatter | solution.py:53
  279.0 1.1 broadcast_in_dim.26
  280.2 22.0 %subtract_select_fusion = (f32[4096,512]{1,0:T(8,128)}, f32[4096,512]{1,0:T(8,128)}, f32[4096,512]{1,0:T(8,128)}) fusion(f32[4096,512]{1,0:T(8,128)} %param.10, pred[512,8,4,128]{3,2,1,0:T(4,128)(4,1)S(1)} %bitcast.95, f32[4096,512]{1,0:T(8,128)} %param.11, bf16[4096,512]{1,0:T(8,128)(2,1)} %reduce-scatter.2.cloned.1.call-done, f32[4096,512]{1,0:T(8,128)} %param.12), kind=kLoop, calls=%fused_computation.1 | loop fusion | flops 35651584 | bytes 56623104 | tf_op jit(solution)/shard_map/jit(_where)/select_n | solution.py:70
  302.1 9.9 %reshape.59 = f32[32,128,4,128]{3,2,1,0:T(4,128)} reshape(f32[4096,512]{1,0:T(8,128)} %get-tuple-element.20) | data formatting | bytes 16777216 | tf_op jit(solution)/shard_map/reshape | solution.py:71
  312.1 11.6 %fusion.7 = bf16[4,6,128,128]{3,1,2,0:T(8,128)(2,1)} fusion(f32[32,128,4,128]{3,2,1,0:T(4,128)} %reshape.59, s32[32]{0:T(128)S(1)} %iota_add_fusion, s32[4,6]{1,0:T(4,128)S(1)} %copy.17, pred[4,6]{1,0:T(4,128)(4,1)S(1)} %iota_compare_fusion), kind=kOutput, calls=%fused_computation.12 | convolution fusion | flops 151389696 | bytes 9175288 | tf_op jit(solution)/shard_map/cjk,kcab->cjab/dot_general | solution.py:72
  323.6 0.0 all-reduce.2.cloned.1.call-update
  323.7 70.7 %all-gather.8.cloned.1.call-done = bf16[256,8192]{1,0:T(8,128)(2,1)} async-done(((bf16[256,512]{1,0:T(8,128)(2,1)}), bf16[256,8192]{1,0:T(8,128)(2,1)}) %all-gather.8.cloned.1.call-update) | async-done | bytes 4194320 | tf_op jit(solution)/shard_map/all_gather | solution.py:31
  394.3 26.9 %all-to-all-done = bf16[16,512,512]{1,2,0:T(8,128)(2,1)} async-done(((bf16[16,512,512]{1,2,0:T(8,128)(2,1)}), bf16[16,512,512]{1,2,0:T(8,128)(2,1)}, u32[]{:S(2)}, u32[]{:S(2)}) %all-to-all-start) | async-done | bytes 8388640 | tf_op jit(solution)/shard_map/all_to_all | solution.py:35
  421.2 7.3 %fusion.10 = bf16[256,512]{0,1:T(8,128)(2,1)S(1)} fusion(bf16[512,8192]{0,1:T(8,128)(2,1)} %bitcast.17, bf16[256,8192]{1,0:T(8,128)(2,1)} %all-gather.8.cloned.1.call-done), kind=kOutput, calls=%fused_computation.15 | convolution fusion | flops 2147614720 | bytes 12845056 | tf_op jit(solution)/shard_map/dot_general | solution.py:38
  428.6 0.8 copy.19
  429.4 7.9 %all-reduce.2.cloned.1.call-done = bf16[4,6,128,128]{3,1,2,0:T(8,128)(2,1)} async-done(((bf16[4,6,128,128]{3,1,2,0:T(8,128)(2,1)}), bf16[4,6,128,128]{3,1,2,0:T(8,128)(2,1)}) %all-reduce.2.cloned.1.call-update) | async-done | bytes 786448 | tf_op jit(solution)/shard_map/psum | solution.py:75
  437.3 2.3 copy.20
  (4 shorter events, 0.0 us)
Async XLA Ops:
  7.2 63.3 %all-gather.4.cloned.1.call-start = ((), (), s32[]{:S(2)}) async-start(), calls=%async_computation.2 | async-start | bytes 4456448 | tf_op jit(solution)/shard_map/all_gather | solution.py:30
  18.0 52.4 %copy-start = (bf16[256,512]{1,0:T(8,128)(2,1)S(1)}, bf16[256,512]{1,0:T(8,128)(2,1)}, u32[]{:S(2)}) copy-start(bf16[256,512]{1,0:T(8,128)(2,1)} %param.9) | copy-start | bytes 786436
  18.0 158.7 %all-gather.6.cloned.1.call-start = ((), (), s32[]{:S(2)}) async-start(), calls=%async_computation.3 | async-start | bytes 12582912 | tf_op jit(solution)/shard_map/all_gather | solution.py:25
  25.4 253.6 %reduce-scatter.2.cloned.1.call-start = ((), (), s32[]{:S(2)}) async-start(), calls=%async_computation.5 | async-start | bytes 12582912 | tf_op jit(solution)/shard_map/reduce_scatter | solution.py:53
  207.1 7.3 %copy-start.1 = (s32[64,64]{1,0:T(8,128)S(1)}, s32[64,64]{1,0:T(8,128)}, u32[]{:S(2)}) copy-start(s32[64,64]{1,0:T(8,128)} %param.13) | copy-start | bytes 49156
  207.1 214.2 %all-to-all-start = ((bf16[16,512,512]{1,2,0:T(8,128)(2,1)}), bf16[16,512,512]{1,2,0:T(8,128)(2,1)}, u32[]{:S(2)}, u32[]{:S(2)}) async-start(bf16[16,512,512]{1,2,0:T(8,128)(2,1)} %fusion.11), calls=%async_computation | async-start | bytes 16777216 | tf_op jit(solution)/shard_map/all_to_all | solution.py:35
  213.5 180.8 %all-gather.8.cloned.1.call-start = ((), (), s32[]{:S(2)}) async-start(), calls=%async_computation.4 | async-start | bytes 4456448 | tf_op jit(solution)/shard_map/all_gather | solution.py:31
  214.1 223.2 %all-reduce.2.cloned.1.call-start = ((), (), s32[]{:S(2)}) async-start(), calls=%async_computation.6 | async-start | bytes 2097152 | tf_op jit(solution)/shard_map/psum | solution.py:75
Sparse Core Ops, SparseCore 0:
  18.2 52.2 all-gather.3
  72.5 104.1 all-gather.5
  179.7 99.3 reduce-scatter.1
  281.0 113.2 all-gather.7
  396.5 40.8 all-reduce.1
